TPU v7x, 1024 devices: a whole 8x8x8 slice. The times are simulated.
1024 devices in a mesh: freq: 32 (over y, x_hi), tm: 32 (over x_lo, z, core).
Axes of the slice: x: 8 (x_hi: 4, x_lo: 2; x = x_hi * 2 + x_lo), y: 8, z: 8, core: 2. Of those that a mesh axis runs over, the one named last changes fastest.
Arguments:
- visibilities: bfloat16 [32, 32, 2, 512, 512], P('freq', 'tm'), may hold values from -1.796875 to 1.796875
- model_vis: bfloat16 [32, 8, 2, 512, 512], P('freq'), may hold values from -0.1796875 to 0.1796875
- station_flags: int32 [32, 32, 512], P('freq', 'tm'), may hold values 0 or 1
- initial_gains: float32 [32, 32, 2, 8, 512], P('freq', 'tm'), may hold values from -6 to 6
- initial_duals: float32 [32, 32, 2, 8, 512], P('freq', 'tm'), may hold values from -1.8 to 1.8
Outputs:
- solved_gains: float32 [32, 32, 2, 8, 512], P('freq', 'tm')
- consensus: float32 [32, 32, 2, 8, 512], P('freq', 'tm')
- final_duals: float32 [32, 32, 2, 8, 512], P('freq', 'tm')
All inputs are finite; a program needn't handle non-finite values. No bound on the sum of `station_flags` on one device may be relied on, other than what follows from the above.
Results may differ from a plain program's by a relative error of at most 0.0003.
Values sent between devices are 32-bit elements; how exact they have to be, the bound alone decides.
A program may use at most 32 MiB of HBM per device.

v0:
```python
import math

import jax
import jax.numpy as jnp
from jax import lax
from jax.sharding import PartitionSpec as P

ITERS = 2


penalty = 1.0


def poly_basis(length, position, order_count):
    centre = position - (length - 1) / 2.0
    constant = jnp.ones_like(position) / math.sqrt(length)
    linear = centre / math.sqrt(length * (length * length - 1) / 12.0)
    stacked = [constant, linear]
    if order_count == 3:
        quadratic = (centre * centre - (length * length - 1) / 12.0) / math.sqrt(
            length * (length * length - 1) * (length * length - 4) / 180.0
        )
        stacked.append(quadratic)
    return jnp.stack(stacked, axis=0)


def local_solve(vis_block, model_block, flag_block, gains_block, target_block):
    real_vis = vis_block[0].astype(jnp.float32)
    imag_vis = vis_block[1].astype(jnp.float32)
    model_real = model_block[:, 0].astype(jnp.float32)
    model_imag = model_block[:, 1].astype(jnp.float32)
    gain_real = gains_block[0]
    gain_imag = gains_block[1]
    weight = flag_block.astype(jnp.float32)
    outer_real = (
        gain_real[:, :, None] * gain_real[:, None, :]
        + gain_imag[:, :, None] * gain_imag[:, None, :]
    )
    outer_imag = (
        gain_imag[:, :, None] * gain_real[:, None, :]
        - gain_real[:, :, None] * gain_imag[:, None, :]
    )
    pred_real = jnp.sum(model_real * outer_real - model_imag * outer_imag, axis=0)
    pred_imag = jnp.sum(model_real * outer_imag + model_imag * outer_real, axis=0)
    pair_weight = weight[:, None] * weight[None, :]
    resid_real = (real_vis - pred_real) * pair_weight
    resid_imag = (imag_vis - pred_imag) * pair_weight
    proj_real = model_real * gain_real[:, None, :] + model_imag * gain_imag[:, None, :]
    proj_imag = model_real * gain_imag[:, None, :] - model_imag * gain_real[:, None, :]
    numer_real = jnp.sum(resid_real[None] * proj_real - resid_imag[None] * proj_imag, axis=2)
    numer_imag = jnp.sum(resid_real[None] * proj_imag + resid_imag[None] * proj_real, axis=2)
    gain_power = (gain_real * gain_real + gain_imag * gain_imag) * weight
    curvature = weight[None, :] * jnp.sum(
        (model_real * model_real + model_imag * model_imag) * gain_power[:, None, :], axis=2
    )
    divisor = curvature + penalty
    new_real = (numer_real + curvature * gain_real + penalty * target_block[0]) / divisor
    new_imag = (numer_imag + curvature * gain_imag + penalty * target_block[1]) / divisor
    return jnp.stack([new_real, new_imag], axis=0)


def polynomial_fit(merged, freq_basis, time_basis):
    products = (
        freq_basis[:, None, None] * time_basis[None, :, None] * merged[None, None, :]
    ).reshape(-1, merged.shape[0])
    totals = lax.psum(products, ("freq", "tm"))
    weights = (freq_basis[:, None] * time_basis[None, :]).reshape(-1)
    return jnp.sum(weights[:, None] * totals, axis=0)


def per_device(visibilities, model_vis, station_flags, initial_gains, initial_duals):
    freq_count = lax.axis_size("freq")
    time_count = lax.axis_size("tm")
    freq_basis = poly_basis(freq_count, lax.axis_index("freq").astype(jnp.float32), 3)
    time_basis = poly_basis(time_count, lax.axis_index("tm").astype(jnp.float32), 2)
    vis_block = visibilities[0, 0]
    model_block = model_vis[0]
    flag_block = station_flags[0, 0]
    current = initial_gains[0, 0]
    scaled_dual = initial_duals[0, 0]
    consensus = current
    for iteration in range(ITERS):
        merged = (current + scaled_dual).reshape(-1)
        consensus = polynomial_fit(merged, freq_basis, time_basis).reshape(current.shape)
        scaled_dual = scaled_dual + current - consensus
        target = consensus - scaled_dual
        current = local_solve(vis_block, model_block, flag_block, current, target)
    return (current[None, None], consensus[None, None], scaled_dual[None, None])


def solution(mesh):
    in_specs = (
        P("freq", "tm", None, None, None),
        P("freq", None, None, None, None),
        P("freq", "tm", None),
        P("freq", "tm", None, None, None),
        P("freq", "tm", None, None, None),
    )
    out_specs = (
        P("freq", "tm", None, None, None),
        P("freq", "tm", None, None, None),
        P("freq", "tm", None, None, None),
    )
    return jax.shard_map(
        per_device, mesh=mesh, in_specs=in_specs, out_specs=out_specs, check_vma=False
    )
```

profile of v0, /device:TPU:1, one launch (start us, length us, event | category | flops | bytes accessed | tf_op | source)
XLA Modules:
  0.0 608.1 jit_solution(9247810146380824009)
XLA Ops:
  7.2 0.0 all-reduce.3.cloned.1.call-start
  7.2 0.9 add.229
  8.1 0.1 pad_maximum_fusion.1
  8.2 0.1 mul.605
  8.3 0.1 mul.606
  8.3 0.1 pad_maximum_fusion.2
  8.4 0.1 mul.608
  8.5 0.1 mul.612
  8.6 0.8 broadcast_multiply_fusion.1
  9.4 0.0 all-reduce.3.cloned.1.call-update
  9.4 0.0 all-reduce.5.cloned.1.call-start
  9.5 0.0 slice-start
  9.5 0.9 slice_bitcast_fusion.3
  10.4 0.9 convert_element_type.69
  11.3 0.7 add_multiply_fusion.1
  12.0 7.2 %fusion.1 = (f32[512,512]{1,0:T(8,128)S(1)}, f32[512,512]{1,0:T(8,128)S(1)}) fusion(f32[8,512]{1,0:T(8,128)S(1)} %get-tuple-element.25, f32[8,512]{1,0:T(8,128)S(1)} %get-tuple-element.24, bf16[8,2,512,512]{3,2,1,0:T(8,128)(2,1)} %bitcast.142), kind=kLoop, calls=%fused_computation.19 | loop fusion | flops 33030144 | bytes 10551296 | tf_op jit(solution)/shard_map/reduce_sum | solution.py:43
  19.2 0.0 copy-start.1
  19.2 0.0 copy-done
  19.2 0.3 multiply_multiply_fusion.3
  19.6 8.8 %subtract_reduce_fusion.1 = (f32[8,512]{1,0:T(8,128)S(1)}, f32[8,512]{1,0:T(8,128)S(1)}, f32[8,512]{1,0:T(8,128)S(1)}) fusion(f32[512,512]{1,0:T(8,128)S(1)} %get-tuple-element.19, f32[512,512]{1,0:T(8,128)S(1)} %get-tuple-element.18, f32[8,512]{1,0:T(8,128)S(1)} %get-tuple-element.25, f32[8,512]{1,0:T(8,128)S(1)} %get-tuple-element.24, ...), kind=kLoop, calls=%fused_computation.38 | loop fusion | flops 44027904 | bytes 10584064 | tf_op jit(solution)/shard_map/reduce_sum | solution.py:50
  28.4 284.8 %all-reduce.3.cloned.1.call-done = f32[6,8192]{1,0:T(8,128)} async-done(((f32[6,8192]{1,0:T(8,128)}), f32[6,8192]{1,0:T(8,128)}) %all-reduce.3.cloned.1.call-update) | async-done | bytes 196624 | tf_op jit(solution)/shard_map/psum | solution.py:66
  313.2 1.1 multiply_reduce_fusion.3
  314.4 0.8 broadcast_multiply_fusion
  315.2 0.0 all-reduce.5.cloned.1.call-update
  315.2 7.0 %fusion.8 = (f32[512,512]{1,0:T(8,128)S(1)}, f32[512,512]{1,0:T(8,128)S(1)}) fusion(f32[8,512]{1,0:T(8,128)S(1)} %get-tuple-element.15, f32[8,512]{1,0:T(8,128)S(1)} %get-tuple-element.14, bf16[8,2,512,512]{3,2,1,0:T(8,128)(2,1)} %bitcast.143), kind=kLoop, calls=%fused_computation.26 | loop fusion | flops 33030144 | bytes 10551296 | tf_op jit(solution)/shard_map/reduce_sum | solution.py:43
  322.3 0.3 multiply_multiply_fusion.1
  322.6 10.7 %subtract_reduce_fusion = (f32[8,512]{1,0:T(8,128)S(1)}, f32[8,512]{1,0:T(8,128)S(1)}, f32[8,512]{1,0:T(8,128)S(1)}) fusion(f32[512,512]{1,0:T(8,128)S(1)} %get-tuple-element.17, f32[512,512]{1,0:T(8,128)S(1)} %get-tuple-element.16, f32[8,512]{1,0:T(8,128)S(1)} %get-tuple-element.15, f32[8,512]{1,0:T(8,128)S(1)} %get-tuple-element.14, ...), kind=kLoop, calls=%fused_computation.33 | loop fusion | flops 44027904 | bytes 10584064 | tf_op jit(solution)/shard_map/reduce_sum | solution.py:50
  333.3 265.5 %all-reduce.5.cloned.1.call-done = f32[6,8192]{1,0:T(8,128)} async-done(((f32[6,8192]{1,0:T(8,128)}), f32[6,8192]{1,0:T(8,128)}) %all-reduce.5.cloned.1.call-update) | async-done | bytes 196624 | tf_op jit(solution)/shard_map/psum | solution.py:66
  598.8 1.1 multiply_reduce_fusion.2
  599.9 0.0 copy-start.2
  600.0 0.6 maximum_bitcast_fusion
  600.6 0.6 fusion.13
  (23 shorter events, 0.2 us)
Async XLA Ops:
  7.2 12.0 %copy-start = (bf16[1,1,2,512,512]{4,3,2,1,0:T(8,128)(2,1)S(1)}, bf16[1,1,2,512,512]{4,3,2,1,0:T(8,128)(2,1)}, u32[]{:S(2)}) copy-start(bf16[1,1,2,512,512]{4,3,2,1,0:T(8,128)(2,1)} %param.5) | copy-start | bytes 3145732
  7.2 306.0 %all-reduce.3.cloned.1.call-start = ((), (), s32[]{:S(2)}) async-start(), calls=%async_computation | async-start | bytes 524288 | tf_op jit(solution)/shard_map/psum | solution.py:66
  9.4 589.4 %all-reduce.5.cloned.1.call-start = ((), (), s32[]{:S(2)}) async-start(), calls=%async_computation.1 | async-start | bytes 524288 | tf_op jit(solution)/shard_map/psum | solution.py:66
  9.5 10.1 %slice-start = ((s8[8388608]{0:T(1024)(128)(4,1)}), s8[4194304]{0:T(1024)(128)(4,1)S(1)}, s32[]{:S(2)}) async-start(s8[8388608]{0:T(1024)(128)(4,1)} %bitcast.145), calls=%async_computation.2 | async-start | bytes 8388608
  12.0 7.5 %slice-start.1 = ((s8[8388608]{0:T(1024)(128)(4,1)}), s8[4194304]{0:T(1024)(128)(4,1)S(1)}, s32[]{:S(2)}) async-start(s8[8388608]{0:T(1024)(128)(4,1)} %bitcast.145), calls=%async_computation.3 | async-start | bytes 8388608
  19.2 295.1 %copy-start.1 = (f32[1,1,2,8,512]{4,3,2,1,0:T(8,128)S(1)}, f32[1,1,2,8,512]{4,3,2,1,0:T(8,128)}, u32[]{:S(2)}) copy-start(f32[1,1,2,8,512]{4,3,2,1,0:T(8,128)} %param.8) | copy-start | bytes 98308
  599.9 1.3 copy-start.2
Sparse Core Ops, SparseCore 0:
  12.7 300.4 all-reduce.2
  317.9 280.8 all-reduce.4
where the time goes:
time: 608 us
  waiting for transfers between devices  550 us (90%)
  other arithmetic  42.1 us (7%)
  between operations  14.3 us (2%)
    psum x2, waiting for transfers between devices, polynomial_fit(): totals = lax.psum(products, ('freq', 'tm'))  550 us
    reduce_sum x2, other arithmetic, local_solve(): jnp.sum(resid_real[None] * proj_real - resid_imag[None] * proj_imag, axis=2)  19.5 us
    reduce_sum x2, other arithmetic, local_solve(): jnp.sum(model_real * outer_real - model_imag * outer_imag, axis=0)  14.2 us
  transfers between devices with their start and end apart: 2, of which 2 were waited for; matrix products, arithmetic and copies ran while one was open for 6% of the time, Pallas kernels for 0%

commit v1 on v0

v1 whole, which is shorter than its diff:
```python
import math

import jax
import jax.numpy as jnp
from jax import lax
from jax.experimental import pallas as pl
from jax.experimental.pallas import tpu as pltpu
from jax.sharding import PartitionSpec as P

DIRS = 8
NR = 512
LANES = 128
TILES = NR // LANES
ROWS = 16
BLOCKS = NR // ROWS
LOADS = 4
N_Y, N_XH, N_XL, N_ZC = 8, 4, 2, 16
N_X = N_XH * N_XL
N_Z = N_ZC // 2
NF = N_Y * N_XH
NT = N_XL * N_ZC
MESH = pl.DeviceIdType.MESH
FAR_FIRST = (4, 3, 5, 2, 6, 1, 7)

F0 = 1.0 / math.sqrt(NF)
F1 = 1.0 / math.sqrt(NF * (NF * NF - 1) / 12.0)
F2 = 1.0 / math.sqrt(NF * (NF * NF - 1) * (NF * NF - 4) / 180.0)
F2_SHIFT = (NF * NF - 1) / 12.0
T0 = 1.0 / math.sqrt(NT)
T1 = 1.0 / math.sqrt(NT * (NT * NT - 1) / 12.0)


def tile(index):
    return pl.ds(index * LANES, LANES)


def to_owner_rows(source, target, first_row):
    for lane_tile in range(TILES):
        for pair in range(DIRS // 2):
            for part in range(2):
                target[lane_tile * 4 + pair, first_row + 2 * part : first_row + 2 * part + 2, :] = source[
                    part, 2 * pair : 2 * pair + 2, tile(lane_tile)
                ]


def from_owner_rows(source, target):
    for lane_tile in range(TILES):
        for pair in range(DIRS // 2):
            for part in range(2):
                target[part, 2 * pair : 2 * pair + 2, tile(lane_tile)] = source[
                    lane_tile * 4 + pair, 2 * part : 2 * part + 2, :
                ]


def add_all(terms):
    while len(terms) > 1:
        terms = [a + b for a, b in zip(terms[::2], terms[1::2])] + terms[len(terms) // 2 * 2 :]
    return terms[0]


def kernel(
    vis_hbm, model_hbm, flag_ref, gains_ref, duals_ref,
    out_gains, out_consensus, out_duals,
    model_v, vis_v, masked_v, column_v, stack_v, d_v, sums_v, numer_v, merged_v, work_v, spare_v, eval_v,
    send_z, recv_z, send_w, recv_w, send_x, recv_x, send_y, recv_y, send_g, recv_g,
    load_sem, z_sem, w_sem, x_sem, y_sem, g_sem,
):
    freq = lax.axis_index("freq")
    time = lax.axis_index("tm")
    y = freq // N_XH
    x_hi = lax.rem(freq, N_XH)
    x_lo = time // N_ZC
    zc = lax.rem(time, N_ZC)
    x = x_hi * N_XL + x_lo
    z = zc // 2
    core = lax.rem(zc, 2)

    def z_peer(step, flip):
        return lax.rem(z + step, N_Z) * 2 + lax.rem(core + flip, 2)

    z_peers = [z_peer(step, flip) for step in FAR_FIRST for flip in (0, 1)] + [z_peer(0, 1)]
    x_peers = [lax.rem(x + step, N_X) for step in FAR_FIRST]
    y_peers = [lax.rem(y + step, N_Y) for step in FAR_FIRST]

    def z_device(peer):
        return (freq, x_lo * N_ZC + peer)

    def x_device(peer):
        return (y * N_XH + peer // N_XL, lax.rem(peer, N_XL) * N_ZC + zc)

    def y_device(peer):
        return (peer * N_XH + x_hi, time)

    loads = []
    for part in range(LOADS):
        rows = pl.ds(part * (NR // LOADS), NR // LOADS)
        model_copy = pltpu.make_async_copy(
            model_hbm.at[0, :, :, rows, :], model_v.at[:, :, rows, :], load_sem.at[0, part]
        )
        vis_copy = pltpu.make_async_copy(vis_hbm.at[0, 0, :, rows, :], vis_v.at[:, rows, :], load_sem.at[1, part])
        model_copy.start()
        vis_copy.start()
        loads.append((model_copy, vis_copy))

    barrier = pltpu.get_barrier_semaphore()
    devices = [z_device(p) for p in z_peers] + [x_device(p) for p in x_peers] + [y_device(p) for p in y_peers]
    for device in devices:
        pl.semaphore_signal(barrier, inc=1, device_id=device, device_id_type=MESH)

    gains = gains_ref[0, 0]
    merged = gains + duals_ref[0, 0]
    merged_v[...] = merged
    to_owner_rows(merged_v, send_z, 0)
    mask = flag_ref[0].astype(jnp.float32)

    pl.semaphore_wait(barrier, len(devices))

    def scatter(source, target, sem, peers, device_of, slot):
        for peer in peers:
            pltpu.make_async_remote_copy(
                src_ref=source(peer),
                dst_ref=target.at[slot],
                send_sem=sem.at[0],
                recv_sem=sem.at[1],
                device_id=device_of(peer),
                device_id_type=MESH,
            ).start()

    def wait_bytes(buffer, count, sem):
        part = buffer.at[pl.ds(0, count)]
        pltpu.make_async_copy(part, part, sem).wait()

    def time_moments(parts):
        total = add_all(list(parts))
        ramp = add_all([(slot - (N_ZC - 1) / 2.0) * part for slot, part in enumerate(parts)])
        shift = (x_lo * N_ZC).astype(jnp.float32) - (NT - N_ZC) / 2.0
        return total * T0, (ramp + shift * total) * T1

    def freq_weights(place):
        centre = place.astype(jnp.float32) - (NF - 1) / 2.0
        return F0, centre * F1, (centre * centre - F2_SHIFT) * F2

    def start_x(turn, parts):
        first, second = time_moments(parts)
        send_x[turn, 0:4, :] = first
        send_x[turn, 4:8, :] = second
        scatter(lambda peer: send_x.at[turn], recv_x.at[turn], x_sem.at[turn], x_peers, x_device, x)
        recv_x[turn, x] = send_x[turn]

    def start_y(turn):
        wait_bytes(recv_x.at[turn], N_X - 1, x_sem.at[turn, 1])
        pairs = [recv_x[turn, N_XL * h] + recv_x[turn, N_XL * h + 1] for h in range(N_XH)]
        weights = [freq_weights(y * N_XH + h) for h in range(N_XH)]
        for order in range(3):
            send_y[turn, order] = add_all([weights[h][order] * pairs[h] for h in range(N_XH)])
        scatter(lambda peer: send_y.at[turn], recv_y.at[turn], y_sem.at[turn], y_peers, y_device, y)
        recv_y[turn, y] = send_y[turn]

    def evaluate(turn):
        wait_bytes(recv_y.at[turn], N_Y - 1, y_sem.at[turn, 1])
        weights = freq_weights(freq)
        coeffs = [add_all([recv_y[turn, h, order] for h in range(N_Y)]) for order in range(3)]
        eval_v[...] = add_all([weights[order] * coeffs[order] for order in range(3)])
        constant = eval_v[0:4, :] * T0
        slope = eval_v[4:8, :] * T1
        shift = (x_lo * N_ZC).astype(jnp.float32) - (NT - 1) / 2.0
        base = constant + shift * slope
        return [base + float(slot) * slope for slot in range(N_ZC)]

    def start_g(turn, values):
        for slot in range(N_ZC):
            send_g[turn, slot] = values[slot]
        scatter(lambda peer: send_g.at[turn, peer], recv_g.at[turn], g_sem.at[turn], z_peers, z_device, zc)
        recv_g[turn, zc] = send_g[turn, zc]

    def consensus_of(turn):
        wait_bytes(recv_g.at[turn], N_ZC - 1, g_sem.at[turn, 1])
        from_owner_rows(recv_g.at[turn], work_v)
        return work_v[...]

    lane = lax.broadcasted_iota(jnp.int32, (ROWS, LANES), 1)
    stack_v[...] = jnp.zeros_like(stack_v)

    def start_solve(current):
        masked_v[...] = current * mask[:, None, :]
        stack_v[0:DIRS, :] = current[0]
        stack_v[DIRS : 2 * DIRS, :] = current[1]
        column_v[...] = jnp.transpose(stack_v[...])

    def solve_rows(first, last):
        def block(index, carry):
            rows = pl.ds(pl.multiple_of(index * ROWS, ROWS), ROWS)
            column = column_v[rows, :]
            resid = []
            for q in range(TILES):
                pred_real = pred_imag = None
                for k in range(DIRS):
                    model_real = model_v[k, 0, rows, tile(q)].astype(jnp.float32)
                    model_imag = model_v[k, 1, rows, tile(q)].astype(jnp.float32)
                    row_real = masked_v[0, k : k + 1, tile(q)]
                    row_imag = masked_v[1, k : k + 1, tile(q)]
                    d_real = model_real * row_real + model_imag * row_imag
                    d_imag = model_imag * row_real - model_real * row_imag
                    d_v[k, 0, :, tile(q)] = d_real
                    d_v[k, 1, :, tile(q)] = d_imag
                    col_real = column[:, k : k + 1]
                    col_imag = column[:, DIRS + k : DIRS + k + 1]
                    term_real = col_real * d_real - col_imag * d_imag
                    term_imag = col_real * d_imag + col_imag * d_real
                    pred_real = term_real if pred_real is None else pred_real + term_real
                    pred_imag = term_imag if pred_imag is None else pred_imag + term_imag
                mask_row = mask[:, q * LANES : (q + 1) * LANES]
                resid.append(
                    (
                        vis_v[0, rows, tile(q)].astype(jnp.float32) * mask_row - pred_real,
                        vis_v[1, rows, tile(q)].astype(jnp.float32) * mask_row - pred_imag,
                    )
                )
            sums = jnp.zeros((ROWS, LANES), jnp.float32)
            for k in range(DIRS):
                numer_real, numer_imag, power = [], [], []
                for q in range(TILES):
                    d_real = d_v[k, 0, :, tile(q)]
                    d_imag = d_v[k, 1, :, tile(q)]
                    resid_real, resid_imag = resid[q]
                    numer_real.append(resid_real * d_real + resid_imag * d_imag)
                    numer_imag.append(resid_imag * d_real - resid_real * d_imag)
                    power.append(d_real * d_real + d_imag * d_imag)
                for place, terms in enumerate((numer_real, numer_imag, power)):
                    total = jnp.sum(add_all(terms), axis=1, keepdims=True)
                    sums = jnp.where(lane == place * DIRS + k, total, sums)
            sums_v[rows, :] = sums
            return carry

        lax.fori_loop(first, last, block, 0)

    def finish_solve(current):
        numer_v[...] = jnp.transpose(sums_v[...])
        curvature = numer_v[2 * DIRS : 3 * DIRS, :] * mask
        weight = 1.0 / (curvature + 1.0)
        return [numer_v[c * DIRS : (c + 1) * DIRS, :] * mask + curvature * current[c] for c in range(2)], weight

    scatter(lambda peer: send_z.at[peer], recv_z, z_sem, z_peers, z_device, zc)
    recv_z[zc] = send_z[zc]
    start_solve(gains)
    per_load = BLOCKS // LOADS
    for part in range(LOADS // 2):
        loads[part][0].wait()
        loads[part][1].wait()
        solve_rows(part * per_load, (part + 1) * per_load)
    wait_bytes(recv_z, N_ZC - 1, z_sem.at[1])
    start_x(0, [recv_z[slot] for slot in range(N_ZC)])
    for part in range(LOADS // 2, LOADS):
        loads[part][0].wait()
        loads[part][1].wait()
        solve_rows(part * per_load, (part + 1) * per_load)
    partial, weight = finish_solve(gains)
    for c in range(2):
        work_v[c] = weight * (partial[c] - merged_v[c]) + merged_v[c]
        spare_v[c] = 2.0 * weight - 1.0
    to_owner_rows(work_v, send_w, 0)
    to_owner_rows(spare_v, send_w, 4)
    scatter(lambda peer: send_w.at[peer], recv_w, w_sem, z_peers, z_device, zc)
    recv_w[zc] = send_w[zc]
    start_y(0)

    values = evaluate(0)
    wait_bytes(recv_w, N_ZC - 1, w_sem.at[1])
    start_x(1, [recv_w[slot, 0:4, :] + recv_w[slot, 4:8, :] * values[slot] for slot in range(N_ZC)])
    start_g(0, values)
    first = consensus_of(0)
    for c in range(2):
        gain = (partial[c] + 2.0 * first[c] - merged_v[c]) * weight
        spare_v[c] = gain
        merged_v[c] = gain + merged_v[c] - first[c]
    start_y(1)
    gains = spare_v[...]
    start_solve(gains)
    solve_rows(0, 3 * BLOCKS // 4)
    start_g(1, evaluate(1))
    solve_rows(3 * BLOCKS // 4, BLOCKS)
    partial, weight = finish_solve(spare_v)
    second = consensus_of(1)
    for c in range(2):
        merged = merged_v[c]
        out_consensus[0, 0, c] = second[c]
        out_duals[0, 0, c] = merged - second[c]
        out_gains[0, 0, c] = (partial[c] + 2.0 * second[c] - merged) * weight

    wait_bytes(recv_z, N_ZC - 1, z_sem.at[0])
    wait_bytes(recv_w, N_ZC - 1, w_sem.at[0])
    for turn in range(2):
        wait_bytes(recv_x.at[turn], N_X - 1, x_sem.at[turn, 0])
        wait_bytes(recv_y.at[turn], N_Y - 1, y_sem.at[turn, 0])
        wait_bytes(recv_g.at[turn], N_ZC - 1, g_sem.at[turn, 0])


def per_device(visibilities, model_vis, station_flags, initial_gains, initial_duals):
    block = jax.ShapeDtypeStruct((1, 1, 2, DIRS, NR), jnp.float32)
    f32 = jnp.float32
    vmem = pl.BlockSpec(memory_space=pltpu.VMEM)
    hbm = pl.BlockSpec(memory_space=pl.ANY)
    return pl.pallas_call(
        kernel,
        out_shape=(block, block, block),
        in_specs=[hbm, hbm, vmem, vmem, vmem],
        out_specs=(vmem, vmem, vmem),
        scratch_shapes=[
            pltpu.VMEM((DIRS, 2, NR, NR), jnp.bfloat16),
            pltpu.VMEM((2, NR, NR), jnp.bfloat16),
            pltpu.VMEM((2, DIRS, NR), f32),
            pltpu.VMEM((NR, LANES), f32),
            pltpu.VMEM((LANES, NR), f32),
            pltpu.VMEM((DIRS, 2, ROWS, NR), f32),
            pltpu.VMEM((NR, LANES), f32),
            pltpu.VMEM((LANES, NR), f32),
            pltpu.VMEM((2, DIRS, NR), f32),
            pltpu.VMEM((2, DIRS, NR), f32),
            pltpu.VMEM((2, DIRS, NR), f32),
            pltpu.VMEM((8, LANES), f32),
            pltpu.VMEM((N_ZC, 4, LANES), f32),
            pltpu.VMEM((N_ZC, 4, LANES), f32),
            pltpu.VMEM((N_ZC, 8, LANES), f32),
            pltpu.VMEM((N_ZC, 8, LANES), f32),
            pltpu.VMEM((2, 8, LANES), f32),
            pltpu.VMEM((2, N_X, 8, LANES), f32),
            pltpu.VMEM((2, 3, 8, LANES), f32),
            pltpu.VMEM((2, N_Y, 3, 8, LANES), f32),
            pltpu.VMEM((2, N_ZC, 4, LANES), f32),
            pltpu.VMEM((2, N_ZC, 4, LANES), f32),
            pltpu.SemaphoreType.DMA((2, LOADS)),
            pltpu.SemaphoreType.DMA((2,)),
            pltpu.SemaphoreType.DMA((2,)),
            pltpu.SemaphoreType.DMA((2, 2)),
            pltpu.SemaphoreType.DMA((2, 2)),
            pltpu.SemaphoreType.DMA((2, 2)),
        ],
        compiler_params=pltpu.CompilerParams(
            collective_id=0, has_side_effects=True, vmem_limit_bytes=60 * 1024 * 1024
        ),
    )(visibilities, model_vis, station_flags, initial_gains, initial_duals)


def solution(mesh):
    in_specs = (
        P("freq", "tm", None, None, None),
        P("freq", None, None, None, None),
        P("freq", "tm", None),
        P("freq", "tm", None, None, None),
        P("freq", "tm", None, None, None),
    )
    out_specs = (P("freq", "tm", None, None, None),) * 3
    return jax.shard_map(per_device, mesh=mesh, in_specs=in_specs, out_specs=out_specs, check_vma=False)
```

time: 608 us -> 63.4 us (0.10)
  waiting for transfers between devices: 550 us -> 0 us
  Pallas kernels: 0 us -> 58.2 us
  other arithmetic: 42.1 us -> 0 us
  between operations: 14.3 us -> 0.64 us
    psum x2 -> x0, waiting for transfers between devices: 550 us -> none  [polynomial_fit(): totals = lax.psum(products, ('freq', 'tm'))]
    pallas_call x0 -> x1, Pallas kernels: none -> 58.2 us  [per_device(): pl.pallas_call(kernel, out_shape=(block, block, block), in_specs=[hbm, hb...]
    reduce_sum x6 -> x0, other arithmetic: 35.9 us -> none  [the longest x2 19.5 us: local_solve(): jnp.sum(resid_real[None] * proj_real - resid_imag[None] * proj_imag, axis=2)]
  transfers between devices with their start and end apart: 2 -> 0, of which waited for: 2 -> 0; matrix products, arithmetic and copies ran while one was open for 6% -> 0% of each run, Pallas kernels for 0% -> 0%
where the time goes in v1:
time: 63.4 us; the launch traced here: 63 us
  Pallas kernels  58.2 us (92%)
  local copies, waits for them, and re-layouts  4.12 us (6%)
  between operations  0.64 us (1%)
    pallas_call x1, Pallas kernels, per_device(): pl.pallas_call(kernel, out_shape=(block, block, block), in_specs=[hbm, hb...  58.2 us
    unnamed x3, local copies, waits for them, and re-layouts  4.12 us

profile of v1, /device:TPU:1, one launch (start us, length us, event | category | flops | bytes accessed | tf_op | source)
XLA Modules:
  0.0 63.0 jit_solution(16329217984273858606)
XLA Ops:
  0.6 58.2 %shard_map.76 = (f32[1,1,2,8,512]{4,3,2,1,0:T(8,128)}, f32[1,1,2,8,512]{4,3,2,1,0:T(8,128)}, f32[1,1,2,8,512]{4,3,2,1,0:T(8,128)}) custom-call(bf16[1,1,2,512,512]{4,3,2,1,0:T(8,128)(2,1)} %vis_hbm.1, bf16[1,8,2,512,512]{4,3,2,1,0:T(8,128)(2,1)} %model_hbm.1, s32[1,1,512]{2,1,0:T(1,128)} %flag_ref.1, f32[1,1,2,8,512]{4,3,2,1,0:T(8,128)} %gains_ref.1, ...), custom_call_target="tpu_custom_call" | custom-call | tf_op jit(solution)/shard_map/pallas_call | solution.py:303
  58.9 1.4 %copy.11 = f32[1,1,2,8,512]{4,3,2,1,0:T(8,128)} copy(f32[1,1,2,8,512]{4,3,2,1,0:T(8,128)} %get-tuple-element.6) | data formatting | bytes 65536
  60.2 1.4 %copy.12 = f32[1,1,2,8,512]{4,3,2,1,0:T(8,128)} copy(f32[1,1,2,8,512]{4,3,2,1,0:T(8,128)} %get-tuple-element.7) | data formatting | bytes 65536
  61.6 1.4 %copy.13 = f32[1,1,2,8,512]{4,3,2,1,0:T(8,128)} copy(f32[1,1,2,8,512]{4,3,2,1,0:T(8,128)} %get-tuple-element.8) | data formatting | bytes 65536

commit v2 on v1

--- a/solution.py
+++ b/solution.py
@@ -20,6 +20,8 @@
 NF = N_Y * N_XH
 NT = N_XL * N_ZC
 MESH = pl.DeviceIdType.MESH
+FIRST_SPAN = 20
+SECOND_SPAN = 18
 FAR_FIRST = (4, 3, 5, 2, 6, 1, 7)
 
 F0 = 1.0 / math.sqrt(NF)
@@ -59,11 +61,12 @@
 
 
 def kernel(
-    vis_hbm, model_hbm, flag_ref, gains_ref, duals_ref,
-    out_gains, out_consensus, out_duals,
-    model_v, vis_v, masked_v, column_v, stack_v, d_v, sums_v, numer_v, merged_v, work_v, spare_v, eval_v,
+    vis_hbm, model_hbm, flag_hbm, gains_hbm, duals_hbm,
+    out_v,
+    model_v, vis_v, wide_v, square_v, flag_v, gains_v, duals_v,
+    masked_v, power_v, column_v, stack_v, d_all, sums_v, numer_v, merged_v, work_v, spare_v, eval_v,
     send_z, recv_z, send_w, recv_w, send_x, recv_x, send_y, recv_y, send_g, recv_g,
-    load_sem, z_sem, w_sem, x_sem, y_sem, g_sem,
+    load_sem, small_sem, z_sem, w_sem, x_sem, y_sem, g_sem,
 ):
     freq = lax.axis_index("freq")
     time = lax.axis_index("tm")
@@ -91,6 +94,18 @@
     def y_device(peer):
         return (peer * N_XH + x_hi, time)
 
+    barrier = pltpu.get_barrier_semaphore()
+    devices = [z_device(p) for p in z_peers] + [x_device(p) for p in x_peers] + [y_device(p) for p in y_peers]
+    small = [
+        pltpu.make_async_copy(gains_hbm.at[0, 0], gains_v, small_sem.at[0]),
+        pltpu.make_async_copy(duals_hbm.at[0, 0], duals_v, small_sem.at[1]),
+        pltpu.make_async_copy(flag_hbm.at[0], flag_v, small_sem.at[2]),
+    ]
+    for copy in small:
+        copy.start()
+    for device in devices:
+        pl.semaphore_signal(barrier, inc=1, device_id=device, device_id_type=MESH)
+
     loads = []
     for part in range(LOADS):
         rows = pl.ds(part * (NR // LOADS), NR // LOADS)
@@ -102,16 +117,11 @@
         vis_copy.start()
         loads.append((model_copy, vis_copy))
 
-    barrier = pltpu.get_barrier_semaphore()
-    devices = [z_device(p) for p in z_peers] + [x_device(p) for p in x_peers] + [y_device(p) for p in y_peers]
-    for device in devices:
-        pl.semaphore_signal(barrier, inc=1, device_id=device, device_id_type=MESH)
-
-    gains = gains_ref[0, 0]
-    merged = gains + duals_ref[0, 0]
-    merged_v[...] = merged
+    for copy in small:
+        copy.wait()
+    merged_v[...] = gains_v[...] + duals_v[...]
     to_owner_rows(merged_v, send_z, 0)
-    mask = flag_ref[0].astype(jnp.float32)
+    mask = flag_v[...].astype(jnp.float32)
 
     pl.semaphore_wait(barrier, len(devices))
 
@@ -151,16 +161,16 @@
         wait_bytes(recv_x.at[turn], N_X - 1, x_sem.at[turn, 1])
         pairs = [recv_x[turn, N_XL * h] + recv_x[turn, N_XL * h + 1] for h in range(N_XH)]
         weights = [freq_weights(y * N_XH + h) for h in range(N_XH)]
-        for order in range(3):
-            send_y[turn, order] = add_all([weights[h][order] * pairs[h] for h in range(N_XH)])
-        scatter(lambda peer: send_y.at[turn], recv_y.at[turn], y_sem.at[turn], y_peers, y_device, y)
-        recv_y[turn, y] = send_y[turn]
+        coeffs = [add_all([weights[h][order] * pairs[h] for h in range(N_XH)]) for order in range(3)]
+        for peer in range(N_Y):
+            there = freq_weights(peer * N_XH + x_hi)
+            send_y[turn, peer] = add_all([there[order] * coeffs[order] for order in range(3)])
+        scatter(lambda peer: send_y.at[turn, peer], recv_y.at[turn], y_sem.at[turn], y_peers, y_device, y)
+        recv_y[turn, y] = send_y[turn, y]
 
     def evaluate(turn):
         wait_bytes(recv_y.at[turn], N_Y - 1, y_sem.at[turn, 1])
-        weights = freq_weights(freq)
-        coeffs = [add_all([recv_y[turn, h, order] for h in range(N_Y)]) for order in range(3)]
-        eval_v[...] = add_all([weights[order] * coeffs[order] for order in range(3)])
+        eval_v[...] = add_all([recv_y[turn, h] for h in range(N_Y)])
         constant = eval_v[0:4, :] * T0
         slope = eval_v[4:8, :] * T1
         shift = (x_lo * N_ZC).astype(jnp.float32) - (NT - 1) / 2.0
@@ -178,25 +188,33 @@
         from_owner_rows(recv_g.at[turn], work_v)
         return work_v[...]
 
-    lane = lax.broadcasted_iota(jnp.int32, (ROWS, LANES), 1)
     stack_v[...] = jnp.zeros_like(stack_v)
+    sums_v[...] = jnp.zeros_like(sums_v)
 
     def start_solve(current):
         masked_v[...] = current * mask[:, None, :]
+        power_v[...] = (current[0] * current[0] + current[1] * current[1]) * mask
         stack_v[0:DIRS, :] = current[0]
         stack_v[DIRS : 2 * DIRS, :] = current[1]
         column_v[...] = jnp.transpose(stack_v[...])
 
-    def solve_rows(first, last):
-        def block(index, carry):
+    def solve_rows(first, last, keep):
+        def block(index, d_v):
             rows = pl.ds(pl.multiple_of(index * ROWS, ROWS), ROWS)
             column = column_v[rows, :]
             resid = []
             for q in range(TILES):
                 pred_real = pred_imag = None
                 for k in range(DIRS):
-                    model_real = model_v[k, 0, rows, tile(q)].astype(jnp.float32)
-                    model_imag = model_v[k, 1, rows, tile(q)].astype(jnp.float32)
+                    if keep:
+                        model_real = model_v[k, 0, rows, tile(q)].astype(jnp.float32)
+                        model_imag = model_v[k, 1, rows, tile(q)].astype(jnp.float32)
+                        wide_v[k, 0, rows, tile(q)] = model_real
+                        wide_v[k, 1, rows, tile(q)] = model_imag
+                        square_v[k, rows, tile(q)] = model_real * model_real + model_imag * model_imag
+                    else:
+                        model_real = wide_v[k, 0, rows, tile(q)]
+                        model_imag = wide_v[k, 1, rows, tile(q)]
                     row_real = masked_v[0, k : k + 1, tile(q)]
                     row_imag = masked_v[1, k : k + 1, tile(q)]
                     d_real = model_real * row_real + model_imag * row_imag
@@ -216,7 +234,6 @@
                         vis_v[1, rows, tile(q)].astype(jnp.float32) * mask_row - pred_imag,
                     )
                 )
-            sums = jnp.zeros((ROWS, LANES), jnp.float32)
             for k in range(DIRS):
                 numer_real, numer_imag, power = [], [], []
                 for q in range(TILES):
@@ -225,14 +242,17 @@
                     resid_real, resid_imag = resid[q]
                     numer_real.append(resid_real * d_real + resid_imag * d_imag)
                     numer_imag.append(resid_imag * d_real - resid_real * d_imag)
-                    power.append(d_real * d_real + d_imag * d_imag)
+                    power.append(square_v[k, rows, tile(q)] * power_v[k : k + 1, tile(q)])
                 for place, terms in enumerate((numer_real, numer_imag, power)):
-                    total = jnp.sum(add_all(terms), axis=1, keepdims=True)
-                    sums = jnp.where(lane == place * DIRS + k, total, sums)
-            sums_v[rows, :] = sums
+                    lane = place * DIRS + k
+                    sums_v[rows, lane : lane + 1] = jnp.sum(add_all(terms), axis=1, keepdims=True)
+
+        def blocks(index, carry):
+            for half in range(2):
+                block(2 * index + half, d_all.at[half])
             return carry
 
-        lax.fori_loop(first, last, block, 0)
+        lax.fori_loop(first // 2, last // 2, blocks, 0)
 
     def finish_solve(current):
         numer_v[...] = jnp.transpose(sums_v[...])
@@ -240,21 +260,25 @@
         weight = 1.0 / (curvature + 1.0)
         return [numer_v[c * DIRS : (c + 1) * DIRS, :] * mask + curvature * current[c] for c in range(2)], weight
 
+    def solve_span(first, last):
+        per_load = BLOCKS // LOADS
+        while first < last:
+            part, offset = divmod(first, per_load)
+            if offset == 0:
+                loads[part][0].wait()
+                loads[part][1].wait()
+            end = min(last, (part + 1) * per_load)
+            solve_rows(first, end, True)
+            first = end
+
     scatter(lambda peer: send_z.at[peer], recv_z, z_sem, z_peers, z_device, zc)
     recv_z[zc] = send_z[zc]
-    start_solve(gains)
-    per_load = BLOCKS // LOADS
-    for part in range(LOADS // 2):
-        loads[part][0].wait()
-        loads[part][1].wait()
-        solve_rows(part * per_load, (part + 1) * per_load)
+    start_solve(gains_v[...])
+    solve_span(0, FIRST_SPAN)
     wait_bytes(recv_z, N_ZC - 1, z_sem.at[1])
     start_x(0, [recv_z[slot] for slot in range(N_ZC)])
-    for part in range(LOADS // 2, LOADS):
-        loads[part][0].wait()
-        loads[part][1].wait()
-        solve_rows(part * per_load, (part + 1) * per_load)
-    partial, weight = finish_solve(gains)
+    solve_span(FIRST_SPAN, BLOCKS)
+    partial, weight = finish_solve(gains_v)
     for c in range(2):
         work_v[c] = weight * (partial[c] - merged_v[c]) + merged_v[c]
         spare_v[c] = 2.0 * weight - 1.0
@@ -265,27 +289,26 @@
     start_y(0)
 
     values = evaluate(0)
+    start_g(0, values)
     wait_bytes(recv_w, N_ZC - 1, w_sem.at[1])
     start_x(1, [recv_w[slot, 0:4, :] + recv_w[slot, 4:8, :] * values[slot] for slot in range(N_ZC)])
-    start_g(0, values)
+    start_y(1)
     first = consensus_of(0)
     for c in range(2):
         gain = (partial[c] + 2.0 * first[c] - merged_v[c]) * weight
         spare_v[c] = gain
         merged_v[c] = gain + merged_v[c] - first[c]
-    start_y(1)
-    gains = spare_v[...]
-    start_solve(gains)
-    solve_rows(0, 3 * BLOCKS // 4)
+    start_solve(spare_v[...])
+    solve_rows(0, SECOND_SPAN, False)
     start_g(1, evaluate(1))
-    solve_rows(3 * BLOCKS // 4, BLOCKS)
+    solve_rows(SECOND_SPAN, BLOCKS, False)
     partial, weight = finish_solve(spare_v)
     second = consensus_of(1)
     for c in range(2):
         merged = merged_v[c]
-        out_consensus[0, 0, c] = second[c]
-        out_duals[0, 0, c] = merged - second[c]
-        out_gains[0, 0, c] = (partial[c] + 2.0 * second[c] - merged) * weight
+        out_v[0, c] = (partial[c] + 2.0 * second[c] - merged) * weight
+        out_v[1, c] = second[c]
+        out_v[2, c] = merged - second[c]
 
     wait_bytes(recv_z, N_ZC - 1, z_sem.at[0])
     wait_bytes(recv_w, N_ZC - 1, w_sem.at[0])
@@ -295,23 +318,39 @@
         wait_bytes(recv_g.at[turn], N_ZC - 1, g_sem.at[turn, 0])
 
 
+def write_outputs(results, gains, consensus, duals, sem):
+    copies = [
+        pltpu.make_async_copy(results.at[place], target.at[0, 0], sem.at[place])
+        for place, target in enumerate((gains, consensus, duals))
+    ]
+    for copy in copies:
+        copy.start()
+    for copy in copies:
+        copy.wait()
+
+
 def per_device(visibilities, model_vis, station_flags, initial_gains, initial_duals):
-    block = jax.ShapeDtypeStruct((1, 1, 2, DIRS, NR), jnp.float32)
     f32 = jnp.float32
     vmem = pl.BlockSpec(memory_space=pltpu.VMEM)
     hbm = pl.BlockSpec(memory_space=pl.ANY)
-    return pl.pallas_call(
+    results = pl.pallas_call(
         kernel,
-        out_shape=(block, block, block),
-        in_specs=[hbm, hbm, vmem, vmem, vmem],
-        out_specs=(vmem, vmem, vmem),
+        out_shape=jax.ShapeDtypeStruct((3, 2, DIRS, NR), f32),
+        in_specs=[hbm] * 5,
+        out_specs=vmem,
         scratch_shapes=[
             pltpu.VMEM((DIRS, 2, NR, NR), jnp.bfloat16),
             pltpu.VMEM((2, NR, NR), jnp.bfloat16),
-            pltpu.VMEM((2, DIRS, NR), f32),
+            pltpu.VMEM((DIRS, 2, NR, NR), f32),
+            pltpu.VMEM((DIRS, NR, NR), f32),
+            pltpu.VMEM((1, NR), jnp.int32),
+            pltpu.VMEM((2, DIRS, NR), f32),
+            pltpu.VMEM((2, DIRS, NR), f32),
+            pltpu.VMEM((2, DIRS, NR), f32),
+            pltpu.VMEM((DIRS, NR), f32),
             pltpu.VMEM((NR, LANES), f32),
             pltpu.VMEM((LANES, NR), f32),
-            pltpu.VMEM((DIRS, 2, ROWS, NR), f32),
+            pltpu.VMEM((2, DIRS, 2, ROWS, NR), f32),
             pltpu.VMEM((NR, LANES), f32),
             pltpu.VMEM((LANES, NR), f32),
             pltpu.VMEM((2, DIRS, NR), f32),
@@ -324,11 +363,12 @@
             pltpu.VMEM((N_ZC, 8, LANES), f32),
             pltpu.VMEM((2, 8, LANES), f32),
             pltpu.VMEM((2, N_X, 8, LANES), f32),
-            pltpu.VMEM((2, 3, 8, LANES), f32),
-            pltpu.VMEM((2, N_Y, 3, 8, LANES), f32),
+            pltpu.VMEM((2, N_Y, 8, LANES), f32),
+            pltpu.VMEM((2, N_Y, 8, LANES), f32),
             pltpu.VMEM((2, N_ZC, 4, LANES), f32),
             pltpu.VMEM((2, N_ZC, 4, LANES), f32),
             pltpu.SemaphoreType.DMA((2, LOADS)),
+            pltpu.SemaphoreType.DMA((3,)),
             pltpu.SemaphoreType.DMA((2,)),
             pltpu.SemaphoreType.DMA((2,)),
             pltpu.SemaphoreType.DMA((2, 2)),
@@ -339,6 +379,15 @@
             collective_id=0, has_side_effects=True, vmem_limit_bytes=60 * 1024 * 1024
         ),
     )(visibilities, model_vis, station_flags, initial_gains, initial_duals)
+    block = jax.ShapeDtypeStruct((1, 1, 2, DIRS, NR), f32)
+    return pl.pallas_call(
+        write_outputs,
+        out_shape=(block, block, block),
+        in_specs=[vmem],
+        out_specs=(hbm, hbm, hbm),
+        scratch_shapes=[pltpu.SemaphoreType.DMA((3,))],
+        compiler_params=pltpu.CompilerParams(vmem_limit_bytes=1024 * 1024),
+    )(results)
 
 
 def solution(mesh):

time: 63.4 us -> 56.7 us (0.89)
  local copies, waits for them, and re-layouts: 4.12 us -> 0.89 us
  Pallas kernels: 58.2 us -> 55 us
    pallas_call x1 -> x2, Pallas kernels: 58.2 us -> 55 us  [the longest x1 54.3 us: per_device(): pl.pallas_call(kernel, out_shape=jax.ShapeDtypeStruct((3, 2, DIRS, NR), f...]
    unnamed x3 -> x2, local copies, waits for them, and re-layouts: 4.12 us -> 0.89 us
where the time goes in v2:
time: 56.7 us; the launch traced here: 56.5 us
  Pallas kernels  55 us (97%)
  local copies, waits for them, and re-layouts  0.89 us (2%)
  between operations  0.65 us (1%)
    pallas_call x1, Pallas kernels, per_device(): pl.pallas_call(kernel, out_shape=jax.ShapeDtypeStruct((3, 2, DIRS, NR), f...  54.3 us

profile of v2, /device:TPU:1, one launch (start us, length us, event | category | flops | bytes accessed | tf_op | source)
XLA Modules:
  0.0 56.5 jit_solution(6726456976970972159)
XLA Ops:
  0.6 54.3 %shard_map.76.results = f32[3,2,8,512]{3,2,1,0:T(8,128)} custom-call(bf16[1,1,2,512,512]{4,3,2,1,0:T(8,128)(2,1)} %vis_hbm.1, bf16[1,8,2,512,512]{4,3,2,1,0:T(8,128)(2,1)} %model_hbm.1, s32[1,1,512]{2,1,0:T(1,128)} %flag_hbm.1, f32[1,1,2,8,512]{4,3,2,1,0:T(8,128)} %gains_hbm.1, f32[1,1,2,8,512]{4,3,2,1,0:T(8,128)} %duals_hbm.1), custom_call_target="tpu_custom_call" | custom-call | tf_op jit(solution)/shard_map/pallas_call | solution.py:336
  54.9 0.0 copy-start
  54.9 0.9 %copy-done = f32[3,2,8,512]{3,2,1,0:T(8,128)S(1)} copy-done((f32[3,2,8,512]{3,2,1,0:T(8,128)S(1)}, f32[3,2,8,512]{3,2,1,0:T(8,128)}, u32[]{:S(2)}) %copy-start) | copy-done | bytes 98328
  55.8 0.7 %shard_map.77 = (f32[1,1,2,8,512]{4,3,2,1,0:T(8,128)}, f32[1,1,2,8,512]{4,3,2,1,0:T(8,128)}, f32[1,1,2,8,512]{4,3,2,1,0:T(8,128)}) custom-call(f32[3,2,8,512]{3,2,1,0:T(8,128)S(1)} %copy-done), custom_call_target="tpu_custom_call" | custom-call | tf_op jit(solution)/shard_map/pallas_call | solution.py:383
Async XLA Ops:
  54.9 0.9 %copy-start = (f32[3,2,8,512]{3,2,1,0:T(8,128)S(1)}, f32[3,2,8,512]{3,2,1,0:T(8,128)}, u32[]{:S(2)}) copy-start(f32[3,2,8,512]{3,2,1,0:T(8,128)} %shard_map.76.results) | copy-start | bytes 294916

commit v3 on v2

--- a/solution.py
+++ b/solution.py
@@ -13,15 +13,14 @@
 TILES = NR // LANES
 ROWS = 16
 BLOCKS = NR // ROWS
-LOADS = 4
 N_Y, N_XH, N_XL, N_ZC = 8, 4, 2, 16
 N_X = N_XH * N_XL
 N_Z = N_ZC // 2
 NF = N_Y * N_XH
 NT = N_XL * N_ZC
 MESH = pl.DeviceIdType.MESH
-FIRST_SPAN = 20
-SECOND_SPAN = 18
+SPANS = (0, 8, 20, 32)
+SECOND_SPAN = 14
 FAR_FIRST = (4, 3, 5, 2, 6, 1, 7)
 
 F0 = 1.0 / math.sqrt(NF)
@@ -107,8 +106,8 @@
         pl.semaphore_signal(barrier, inc=1, device_id=device, device_id_type=MESH)
 
     loads = []
-    for part in range(LOADS):
-        rows = pl.ds(part * (NR // LOADS), NR // LOADS)
+    for part, (start, end) in enumerate(zip(SPANS, SPANS[1:])):
+        rows = pl.ds(start * ROWS, (end - start) * ROWS)
         model_copy = pltpu.make_async_copy(
             model_hbm.at[0, :, :, rows, :], model_v.at[:, :, rows, :], load_sem.at[0, part]
         )
@@ -260,24 +259,19 @@
         weight = 1.0 / (curvature + 1.0)
         return [numer_v[c * DIRS : (c + 1) * DIRS, :] * mask + curvature * current[c] for c in range(2)], weight
 
-    def solve_span(first, last):
-        per_load = BLOCKS // LOADS
-        while first < last:
-            part, offset = divmod(first, per_load)
-            if offset == 0:
-                loads[part][0].wait()
-                loads[part][1].wait()
-            end = min(last, (part + 1) * per_load)
-            solve_rows(first, end, True)
-            first = end
+    def solve_span(part):
+        loads[part][0].wait()
+        loads[part][1].wait()
+        solve_rows(SPANS[part], SPANS[part + 1], True)
 
     scatter(lambda peer: send_z.at[peer], recv_z, z_sem, z_peers, z_device, zc)
     recv_z[zc] = send_z[zc]
     start_solve(gains_v[...])
-    solve_span(0, FIRST_SPAN)
+    solve_span(0)
+    solve_span(1)
     wait_bytes(recv_z, N_ZC - 1, z_sem.at[1])
     start_x(0, [recv_z[slot] for slot in range(N_ZC)])
-    solve_span(FIRST_SPAN, BLOCKS)
+    solve_span(2)
     partial, weight = finish_solve(gains_v)
     for c in range(2):
         work_v[c] = weight * (partial[c] - merged_v[c]) + merged_v[c]
@@ -332,7 +326,11 @@
 def per_device(visibilities, model_vis, station_flags, initial_gains, initial_duals):
     f32 = jnp.float32
     vmem = pl.BlockSpec(memory_space=pltpu.VMEM)
-    hbm = pl.BlockSpec(memory_space=pl.ANY)
+    hbm = pl.BlockSpec(memory_space=pltpu.HBM)
+    visibilities, model_vis, station_flags, initial_gains, initial_duals = (
+        pltpu.with_memory_space_constraint(array, pltpu.HBM)
+        for array in (visibilities, model_vis, station_flags, initial_gains, initial_duals)
+    )
     results = pl.pallas_call(
         kernel,
         out_shape=jax.ShapeDtypeStruct((3, 2, DIRS, NR), f32),
@@ -367,7 +365,7 @@
             pltpu.VMEM((2, N_Y, 8, LANES), f32),
             pltpu.VMEM((2, N_ZC, 4, LANES), f32),
             pltpu.VMEM((2, N_ZC, 4, LANES), f32),
-            pltpu.SemaphoreType.DMA((2, LOADS)),
+            pltpu.SemaphoreType.DMA((2, len(SPANS) - 1)),
             pltpu.SemaphoreType.DMA((3,)),
             pltpu.SemaphoreType.DMA((2,)),
             pltpu.SemaphoreType.DMA((2,)),
@@ -376,7 +374,7 @@
             pltpu.SemaphoreType.DMA((2, 2)),
         ],
         compiler_params=pltpu.CompilerParams(
-            collective_id=0, has_side_effects=True, vmem_limit_bytes=60 * 1024 * 1024
+            collective_id=0, has_side_effects=True, vmem_limit_bytes=44 * 1024 * 1024
         ),
     )(visibilities, model_vis, station_flags, initial_gains, initial_duals)
     block = jax.ShapeDtypeStruct((1, 1, 2, DIRS, NR), f32)

time: 56.7 us -> 54.4 us (0.959)
  Pallas kernels: 55 us -> 53.6 us
  local copies, waits for them, and re-layouts: 0.89 us -> 0 us
    pallas_call x1, Pallas kernels: 54.3 us -> 53 us  [per_device(): pl.pallas_call(kernel, out_shape=jax.ShapeDtypeStruct((3, 2, DIRS, NR), f...]
    unnamed x2 -> x0, local copies, waits for them, and re-layouts: 0.89 us -> none
where the time goes in v3:
time: 54.4 us; the launch traced here: 54.3 us
  Pallas kernels  53.6 us (99%)
  between operations  0.64 us (1%)
    pallas_call x1, Pallas kernels, per_device(): pl.pallas_call(kernel, out_shape=jax.ShapeDtypeStruct((3, 2, DIRS, NR), f...  53 us

profile of v3, /device:TPU:1, one launch (start us, length us, event | category | flops | bytes accessed | tf_op | source)
XLA Modules:
  0.0 54.3 jit_solution(11683099182333832538)
XLA Ops:
  0.6 53.0 %shard_map.76.results = f32[3,2,8,512]{3,2,1,0:T(8,128)S(1)} custom-call(bf16[1,1,2,512,512]{4,3,2,1,0:T(8,128)(2,1)} %vis_hbm.1, bf16[1,8,2,512,512]{4,3,2,1,0:T(8,128)(2,1)} %model_hbm.1, s32[1,1,512]{2,1,0:T(1,128)} %flag_hbm.1, f32[1,1,2,8,512]{4,3,2,1,0:T(8,128)} %gains_hbm.1, f32[1,1,2,8,512]{4,3,2,1,0:T(8,128)} %duals_hbm.1), custom_call_target="tpu_custom_call" | custom-call | tf_op jit(solution)/shard_map/pallas_call | solution.py:334
  53.6 0.7 %shard_map.77 = (f32[1,1,2,8,512]{4,3,2,1,0:T(8,128)}, f32[1,1,2,8,512]{4,3,2,1,0:T(8,128)}, f32[1,1,2,8,512]{4,3,2,1,0:T(8,128)}) custom-call(f32[3,2,8,512]{3,2,1,0:T(8,128)S(1)} %shard_map.76.results), custom_call_target="tpu_custom_call" | custom-call | tf_op jit(solution)/shard_map/pallas_call | solution.py:381
